TPU v7x, 32 devices: a whole 2x2x4 slice. The times are simulated.
32 devices in a mesh: section: 2 (over core), row: 4 (over y, x), col: 4 (over z).
Axes of the slice: x: 2, y: 2, z: 4, core: 2. Of those that a mesh axis runs over, the one named last changes fastest.
Arguments:
- out_grad: bfloat16 [2048, 256], P(('row', 'col')), may hold values from -6 to 6
- pre_act: bfloat16 [2, 2048, 256], P('section', ('row', 'col')), may hold values from -6 to 6
- aggregated: bfloat16 [2, 2048, 256], P('section', ('row', 'col')), may hold values from -6 to 6
- weights: bfloat16 [2, 256, 256], P('section'), may hold values from -0.375 to 0.375
- tiles: bfloat16 [4, 4, 64, 128, 128], P('row', 'col'), may hold values from -0.109375 to 0.109375
- tile_index: int32 [4, 4, 64, 2], P('row', 'col'), may hold values from 0 to 3, as said below
- live_count: int32 [4, 4], P('row', 'col'), may hold values from 8 to 64, as said below
Outputs:
- weight_grad: float32 [2, 256, 256], P('section')
- feature_grads: bfloat16 [2, 2048, 256], P('section', ('row', 'col'))
Inputs may be any that keep to these rules, and one draw needn't show every extreme that they name: `tile_index`: both entries index blocks of the tile: the first is under 4, the second under 4. `live_count`: some tile uses all 64 slots.
All inputs are finite; a program needn't handle non-finite values.
Results may differ from a plain program's by a relative error of at most 0.012.
Values may be sent and summed in bfloat16 or wider, within the bound.
A program may use at most 64 MiB of HBM per device.

v0:
```python
import math
import jax
import jax.numpy as jnp
from jax import lax
from jax.sharding import PartitionSpec as P


def from_behind(value, axis, steps):
    count = lax.axis_size(axis)
    leading, last = (max(0, -steps), min(count, count - steps))
    return lax.ppermute(value, axis, [(source, source + steps) for source in range(leading, last)])


def on_device(out_grad, pre_act, aggregated, weights, tiles, tile_index, live_count):
    section_id = lax.axis_index("section")
    upper = section_id == 1
    pre_layer = pre_act[0]
    saved_agg = aggregated[0]
    weight_mat = weights[0]
    tile_blocks = tiles[0, 0]
    tile_slots = tile_index[0, 0]
    tile_count = live_count[0, 0]
    node_rows = out_grad.shape[0]
    width = out_grad.shape[1]
    slot_total = tile_blocks.shape[0]
    block = tile_blocks.shape[1]
    tile_rows = node_rows * lax.axis_size("col")
    row_blocks = tile_rows // block
    group = min(32, slot_total)
    groups = slot_total // group
    grouped_slots = tile_slots.reshape(groups, group, 2)
    all_targets = jnp.arange(row_blocks, dtype=jnp.int32)

    def spread(row_grad):
        return lax.all_gather(row_grad, "row", axis=0, tiled=True)

    def block_total(source, col_blocks):
        height = source.shape[1]
        grouped_blocks = source.reshape(groups, group, height, block)

        def group_term(total, blocks_here, slots_here, first_slot):
            picked = jnp.take(col_blocks, slots_here[:, 1], axis=0)
            products = jnp.einsum(
                "sij,sjf->sif", blocks_here, picked, preferred_element_type=jnp.float32
            )
            slot_ids = first_slot + jnp.arange(group, dtype=jnp.int32)
            live = slot_ids < tile_count
            select = ((slots_here[:, 0][None, :] == all_targets[:, None]) & live[None, :]).astype(
                jnp.float32
            )
            return total + jnp.einsum("bs,sif->bif", select, products)

        start_total = jnp.zeros((row_blocks, height, width), jnp.float32)

        def scan_step(total, group_id):
            blocks_here = lax.dynamic_index_in_dim(grouped_blocks, group_id, 0, False)
            slots_here = lax.dynamic_index_in_dim(grouped_slots, group_id, 0, False)
            return (group_term(total, blocks_here, slots_here, group_id * group), None)

        total, _ = lax.scan(scan_step, start_total, jnp.arange(groups, dtype=jnp.int32))
        return total.reshape(row_blocks * height, width)

    def reduce_col(source, gathered):
        col_blocks = gathered.reshape(-1, block, width)
        height = source.shape[1]
        return lax.psum_scatter(
            block_total(source, col_blocks), "col", scatter_dimension=0, tiled=True
        )

    def local_terms(incoming):
        masked = jnp.where(pre_layer > 0, incoming, jnp.zeros_like(incoming))
        weight_term = lax.dot_general(
            saved_agg, masked, (((0,), (0,)), ((), ())), preferred_element_type=jnp.float32
        )
        row_grad = lax.dot_general(
            masked, weight_mat, (((1,), (1,)), ((), ())), preferred_element_type=jnp.float32
        ).astype(jnp.bfloat16)
        return (weight_term, row_grad)

    def backward_step(incoming):
        weight_term, row_grad = local_terms(incoming)
        summed = reduce_col(tile_blocks, spread(row_grad))
        return (weight_term, summed.astype(jnp.bfloat16))

    first_input = jnp.where(upper, out_grad, jnp.zeros_like(out_grad))
    first_weight, first_grad = backward_step(first_input)
    received = from_behind(first_grad, "section", -1)
    second_weight, second_grad = backward_step(received)
    local_weight = jnp.where(upper, first_weight, second_weight)
    feature_block = jnp.where(upper, first_grad, second_grad)
    total_weight = lax.psum(local_weight, ("row", "col"))
    node_total = node_rows * lax.axis_size("row") * lax.axis_size("col")
    weight_grad = (total_weight * (1.0 / math.sqrt(node_total)))[None]
    return (weight_grad, feature_block[None])


def solution(mesh):
    placed = (
        P(("row", "col"), None),
        P("section", ("row", "col"), None),
        P("section", ("row", "col"), None),
        P("section", None, None),
        P("row", "col", None, None, None),
        P("row", "col", None, None),
        P("row", "col"),
    )
    return jax.shard_map(
        on_device,
        mesh=mesh,
        in_specs=placed,
        out_specs=(P("section", None, None), P("section", ("row", "col"), None)),
        check_vma=False,
    )
```

profile of v0, /device:TPU:0, one launch (start us, length us, event | category | flops | bytes accessed | tf_op | source)
XLA Modules:
  0.0 212.3 jit_solution(15838875846190478118)
XLA Ops:
  8.3 10.5 %all_gather.6 = bf16[512,256]{1,0:T(8,128)(2,1)S(1)} all-gather(bf16[128,256]{1,0:T(8,128)(2,1)S(1)} %convolution_convert_fusion.1), channel_id=1, replica_groups=mesh['section'=2,'row'=4,'col'=4] {'row'}, dimensions={0}, use_global_device_ids=true | all-gather | bytes 327680 | tf_op jit(solution)/shard_map/all_gather | solution.py:35
  19.6 20.1 %while.22 = (s32[]{:T(128)}, f32[4,128,256]{2,0,1:T(4,128)S(1)}, s32[2]{0:T(128)S(1)}, s32[2,32,2]{1,2,0:T(2,128)S(1)}, s32[]{:T(128)}, /*index=5*/bf16[2,32,128...) while((s32[]{:T(128)}, f32[4,128,256]{2,0,1:T(4,128)S(1)}, ...), condition=%wide.region_1.3_spmd.clone, body=%wide.region_0.2_spmd.clone.sunk | while | flops 278136320 | bytes 12588737 | solution.py:60
  22.2 2.0 gather_fusion
  24.2 2.7 %fusion.70 = bf16[32,128,256]{2,1,0:T(8,128)(2,1)S(1)} fusion(bf16[32,128,256]{2,1,0:T(8,128)(2,1)} %gather_fusion, pred[32]{0:T(512)(128)(4,1)S(1)} %get-tuple-element.273, bf16[2,32,128,128]{3,2,1,0:T(8,128)(2,1)} %get-tuple-element.310, s32[]{:T(128)S(6)} %select_n.94), kind=kOutput, calls=%fused_computation.6.clone.1 | convolution fusion | flops 269484032 | bytes 5242916 | tf_op jit(solution)/shard_map/while/body/eval_jaxpr/sij,sjf->sif/dot_general | solution.py:43
  28.2 1.4 fusion.71
  32.3 2.0 gather_fusion
  34.3 2.7 %fusion.70 = bf16[32,128,256]{2,1,0:T(8,128)(2,1)S(1)} fusion(bf16[32,128,256]{2,1,0:T(8,128)(2,1)} %gather_fusion, pred[32]{0:T(512)(128)(4,1)S(1)} %get-tuple-element.273, bf16[2,32,128,128]{3,2,1,0:T(8,128)(2,1)} %get-tuple-element.310, s32[]{:T(128)S(6)} %select_n.94), kind=kOutput, calls=%fused_computation.6.clone.1 | convolution fusion | flops 269484032 | bytes 5242916 | tf_op jit(solution)/shard_map/while/body/eval_jaxpr/sij,sjf->sif/dot_general | solution.py:43
  38.3 1.4 fusion.71
  40.7 22.0 %reduce-scatter.3.cloned.1.call-done = f32[128,256]{1,0:T(8,128)} async-done(((f32[512,256]{1,0:T(8,128)}), f32[128,256]{1,0:T(8,128)}) %reduce-scatter.3.cloned.1.call-update) | async-done | bytes 131088 | tf_op jit(solution)/shard_map/reduce_scatter | solution.py:66
  63.7 1.3 collective-permute-start
  65.2 1.6 collective-permute-done
  67.0 8.9 %all_gather.7 = bf16[512,256]{1,0:T(8,128)(2,1)S(1)} all-gather(bf16[128,256]{1,0:T(8,128)(2,1)S(1)} %convolution_convert_fusion), channel_id=1, replica_groups=mesh['section'=2,'row'=4,'col'=4] {'row'}, dimensions={0}, use_global_device_ids=true | all-gather | bytes 327680 | tf_op jit(solution)/shard_map/all_gather | solution.py:35
  75.9 0.9 fusion.40
  77.0 19.5 %while.23 = (s32[]{:T(128)}, f32[4,128,256]{2,0,1:T(4,128)S(1)}, s32[2]{0:T(128)S(1)}, s32[2,32,2]{1,2,0:T(2,128)S(1)}, s32[]{:T(128)}, /*index=5*/bf16[2,32,128...) while((s32[]{:T(128)}, f32[4,128,256]{2,0,1:T(4,128)S(1)}, ...), condition=%wide.region_5.7_spmd.clone, body=%wide.region_4.6_spmd.clone.sunk | while | flops 278136320 | bytes 12588737 | solution.py:60
  79.3 2.0 gather_fusion.1
  81.3 2.7 %fusion.76 = bf16[32,128,256]{2,1,0:T(8,128)(2,1)S(1)} fusion(bf16[32,128,256]{2,1,0:T(8,128)(2,1)} %gather_fusion.1, pred[32]{0:T(512)(128)(4,1)S(1)} %get-tuple-element.282, bf16[2,32,128,128]{3,2,1,0:T(8,128)(2,1)} %get-tuple-element.343, s32[]{:T(128)S(6)} %select_n.96), kind=kOutput, calls=%fused_computation.28.clone.1 | convolution fusion | flops 269484032 | bytes 5242916 | tf_op jit(solution)/shard_map/while/body/eval_jaxpr/sij,sjf->sif/dot_general | solution.py:43
  85.2 1.4 fusion.77
  89.0 2.0 gather_fusion.1
  91.0 2.7 %fusion.76 = bf16[32,128,256]{2,1,0:T(8,128)(2,1)S(1)} fusion(bf16[32,128,256]{2,1,0:T(8,128)(2,1)} %gather_fusion.1, pred[32]{0:T(512)(128)(4,1)S(1)} %get-tuple-element.282, bf16[2,32,128,128]{3,2,1,0:T(8,128)(2,1)} %get-tuple-element.343, s32[]{:T(128)S(6)} %select_n.96), kind=kOutput, calls=%fused_computation.28.clone.1 | convolution fusion | flops 269484032 | bytes 5242916 | tf_op jit(solution)/shard_map/while/body/eval_jaxpr/sij,sjf->sif/dot_general | solution.py:43
  95.0 1.4 fusion.77
  97.3 83.9 %all-reduce.2.cloned.1.call-done = f32[256,256]{0,1:T(8,128)} async-done(((f32[256,256]{0,1:T(8,128)}), f32[256,256]{0,1:T(8,128)}) %all-reduce.2.cloned.1.call-update) | async-done | bytes 262160 | tf_op jit(solution)/shard_map/psum | solution.py:91
  181.2 1.0 multiply_bitcast_fusion
  183.0 21.3 %reduce-scatter.5.cloned.1.call-done = f32[128,256]{1,0:T(8,128)} async-done(((f32[512,256]{1,0:T(8,128)}), f32[128,256]{1,0:T(8,128)}) %reduce-scatter.5.cloned.1.call-update) | async-done | bytes 131088 | tf_op jit(solution)/shard_map/reduce_scatter | solution.py:66
  204.3 1.5 select_bitcast_fusion
  (52 shorter events, 11.0 us)
Async XLA Ops:
  7.2 0.9 copy-start
  7.2 55.6 %reduce-scatter.3.cloned.1.call-start = ((), (), s32[]{:S(2)}) async-start(), calls=%async_computation.2 | async-start | bytes 655360 | tf_op jit(solution)/shard_map/reduce_scatter | solution.py:66
  19.6 45.4 %copy-start.2 = (bf16[1,128,256]{2,1,0:T(8,128)(2,1)S(1)}, bf16[1,128,256]{2,1,0:T(8,128)(2,1)}, u32[]{:S(2)}) copy-start(bf16[1,128,256]{2,1,0:T(8,128)(2,1)} %param.15) | copy-start | bytes 196612
  19.6 45.4 %copy-start.3 = (bf16[128,256]{1,0:T(8,128)(2,1)S(1)}, bf16[128,256]{1,0:T(8,128)(2,1)}, u32[]{:S(2)}) copy-start(bf16[128,256]{1,0:T(8,128)(2,1)} %param.13) | copy-start | bytes 196612
  40.7 140.5 %all-reduce.2.cloned.1.call-start = ((), (), s32[]{:S(2)}) async-start(), calls=%async_computation.3 | async-start | bytes 524288 | tf_op jit(solution)/shard_map/psum | solution.py:91
  63.7 3.1 %collective-permute-start = (bf16[128,256]{1,0:T(8,128)(2,1)S(1)}, bf16[128,256]{1,0:T(8,128)(2,1)S(1)}, u32[]{:S(2)}, u32[]{:S(2)}) collective-permute-start(bf16[128,256]{1,0:T(8,128)(2,1)S(1)} %convert_element_type.15), channel_id=1, source_target_pairs={{16,0},{17,1},{18,2},{19,3},{20,4},{21,5},{22,6},{23,7},{24,8},{25... | collective-permute-start | bytes 196616 | tf_op jit(solution)/shard_map/ppermute | solution.py:11
  76.9 127.4 %reduce-scatter.5.cloned.1.call-start = ((), (), s32[]{:S(2)}) async-start(), calls=%async_computation.4 | async-start | bytes 655360 | tf_op jit(solution)/shard_map/reduce_scatter | solution.py:66
  96.4 107.9 %copy-start.1 = (f32[128,256]{1,0:T(8,128)S(1)}, f32[128,256]{1,0:T(8,128)}, u32[]{:S(2)}) copy-start(f32[128,256]{1,0:T(8,128)} %reduce-scatter.3.cloned.1.call-done) | copy-start | bytes 393220
Sparse Core Ops, SparseCore 0:
  40.8 21.9 reduce-scatter.2
  77.0 104.1 all-reduce.1
  183.6 20.6 reduce-scatter.4
where the time goes:
time: 213 us; the launch traced here: 212 us
  waiting for transfers between devices  129 us (61%)
  blocking collectives  19.4 us (9%)
  matrix products  18.1 us (8%)
  local copies, waits for them, and re-layouts  13.9 us (7%)
  between operations  13.9 us (7%)
  loops' own time  9.92 us (5%)
  other arithmetic  6.98 us (3%)
    psum x1, waiting for transfers between devices, on_device(): total_weight = lax.psum(local_weight, ('row', 'col'))  83.9 us
    reduce_scatter x2, waiting for transfers between devices, reduce_col(): lax.psum_scatter(block_total(source, col_blocks), 'col', scatter_dimensio...  43.3 us
    all_gather x2, blocking collectives, spread(): return lax.all_gather(row_grad, 'row', axis=0, tiled=True)  19.4 us
    dot_general x4, matrix products, group_term(): jnp.einsum('sij,sjf->sif', blocks_here, picked, preferred_element_type=jn...  10.8 us
    another operation x2, loops' own time, block_total(): lax.scan(scan_step, start_total, jnp.arange(groups, dtype=jnp.int32))  9.92 us
    gather x4, local copies, waits for them, and re-layouts, group_term(): picked = jnp.take(col_blocks, slots_here[:, 1], axis=0)  8.08 us
    dot_general x4, matrix products, group_term(): return total + jnp.einsum('bs,sif->bif', select, products)  5.75 us
  transfers between devices with their start and end apart: 4, of which 4 were waited for; matrix products, arithmetic and copies ran while one was open for 8% of the time, Pallas kernels for 0%

commit v1 on v0

--- a/solution.py
+++ b/solution.py
@@ -3,6 +3,18 @@
 import jax.numpy as jnp
 from jax import lax
 from jax.sharding import PartitionSpec as P
+
+
+def doubled_up(array, axis, dim):
+    ways, here = (lax.axis_size(axis), lax.axis_index(axis))
+    grown, reach = (array, 1)
+    while reach < ways:
+        theirs = lax.ppermute(grown, axis, [(d, d ^ reach) for d in range(ways)])
+        mine_first = jnp.concatenate([grown, theirs], axis=dim)
+        theirs_first = jnp.concatenate([theirs, grown], axis=dim)
+        grown = jnp.where(here & reach == 0, mine_first, theirs_first)
+        reach = 2 * reach
+    return grown
 
 
 def from_behind(value, axis, steps):
@@ -32,7 +44,7 @@
     all_targets = jnp.arange(row_blocks, dtype=jnp.int32)
 
     def spread(row_grad):
-        return lax.all_gather(row_grad, "row", axis=0, tiled=True)
+        return doubled_up(row_grad, "row", 0)
 
     def block_total(source, col_blocks):
         height = source.shape[1]

time: 213 us -> 211 us (level)
  blocking collectives: 19.4 us -> 0 us
  waiting for transfers between devices: 129 us -> 138 us
  starting transfers between devices: 1.41 us -> 9.26 us
    all_gather x2 -> x0, blocking collectives: 19.4 us -> none  [spread(): return lax.all_gather(row_grad, 'row', axis=0, tiled=True)]
    ppermute x0 -> x4, waiting for transfers between devices: none -> 11 us  [doubled_up(): theirs = lax.ppermute(grown, axis, [(d, d ^ reach) for d in range(ways)])]
    ppermute x0 -> x4, starting transfers between devices: none -> 7.85 us  [doubled_up(): theirs = lax.ppermute(grown, axis, [(d, d ^ reach) for d in range(ways)])]
    psum x1, waiting for transfers between devices: 83.9 us -> 80.6 us  [on_device(): total_weight = lax.psum(local_weight, ('row', 'col'))]
  transfers between devices with their start and end apart: 4 -> 8, of which waited for: 4 -> 8; matrix products, arithmetic and copies ran while one was open for 8% -> 9% of each run, Pallas kernels for 0% -> 0%
where the time goes in v1:
time: 211 us
  waiting for transfers between devices  138 us (65%)
  matrix products  18.1 us (9%)
  local copies, waits for them, and re-layouts  14 us (7%)
  between operations  13.9 us (7%)
  loops' own time  10.5 us (5%)
  starting transfers between devices  9.26 us (4%)
  other arithmetic  7.27 us (3%)
    psum x1, waiting for transfers between devices, on_device(): total_weight = lax.psum(local_weight, ('row', 'col'))  80.6 us
    reduce_scatter x2, waiting for transfers between devices, reduce_col(): lax.psum_scatter(block_total(source, col_blocks), 'col', scatter_dimensio...  44.2 us
    ppermute x4, waiting for transfers between devices, doubled_up(): theirs = lax.ppermute(grown, axis, [(d, d ^ reach) for d in range(ways)])  11 us
    dot_general x4, matrix products, group_term(): jnp.einsum('sij,sjf->sif', blocks_here, picked, preferred_element_type=jn...  10.8 us
    another operation x2, loops' own time, block_total(): lax.scan(scan_step, start_total, jnp.arange(groups, dtype=jnp.int32))  10.5 us
    gather x4, local copies, waits for them, and re-layouts, group_term(): picked = jnp.take(col_blocks, slots_here[:, 1], axis=0)  8.03 us
    ppermute x4, starting transfers between devices, doubled_up(): theirs = lax.ppermute(grown, axis, [(d, d ^ reach) for d in range(ways)])  7.85 us
    dot_general x4, matrix products, group_term(): return total + jnp.einsum('bs,sif->bif', select, products)  5.75 us
  transfers between devices with their start and end apart: 8, of which 8 were waited for; matrix products, arithmetic and copies ran while one was open for 9% of the time, Pallas kernels for 0%

profile of v1, /device:TPU:0, one launch (start us, length us, event | category | flops | bytes accessed | tf_op | source)
XLA Modules:
  0.0 210.6 jit_solution(14920768915160429717)
XLA Ops:
  8.3 3.0 %collective-permute-start = (bf16[128,256]{1,0:T(8,128)(2,1)S(1)}, bf16[128,256]{1,0:T(8,128)(2,1)S(1)}, u32[]{:S(2)}, u32[]{:S(2)}) collective-permute-start(bf16[128,256]{1,0:T(8,128)(2,1)S(1)} %convolution_convert_fusion.1), channel_id=1, source_target_pairs={{0,4},{4,0},{8,12},{12,8},{1,5},{5,1},{9,13},{13,9},{2,6},{6,2},{1... | collective-permute-start | bytes 196616 | tf_op jit(solution)/shard_map/ppermute | solution.py:12
  11.3 2.9 %collective-permute-done = bf16[128,256]{1,0:T(8,128)(2,1)S(1)} collective-permute-done((bf16[128,256]{1,0:T(8,128)(2,1)S(1)}, bf16[128,256]{1,0:T(8,128)(2,1)S(1)}, u32[]{:S(2)}, u32[]{:S(2)}) %collective-permute-start) | collective-permute-done | bytes 65568 | tf_op jit(solution)/shard_map/ppermute | solution.py:12
  14.3 1.8 collective-permute-start.1
  16.9 3.0 %collective-permute-done.1 = bf16[256,256]{1,0:T(8,128)(2,1)S(1)} collective-permute-done((bf16[256,256]{1,0:T(8,128)(2,1)S(1)}, bf16[256,256]{1,0:T(8,128)(2,1)S(1)}, u32[]{:S(2)}, u32[]{:S(2)}) %collective-permute-start.1) | collective-permute-done | bytes 131104 | tf_op jit(solution)/shard_map/ppermute | solution.py:12
  20.0 20.1 %while.22 = (s32[]{:T(128)}, f32[4,128,256]{2,0,1:T(4,128)S(1)}, s32[2]{0:T(128)S(1)}, s32[2,32,2]{1,2,0:T(2,128)S(1)}, s32[]{:T(128)}, /*index=5*/bf16[2,32,128...) while((s32[]{:T(128)}, f32[4,128,256]{2,0,1:T(4,128)S(1)}, ...), condition=%wide.region_1.3_spmd.clone, body=%wide.region_0.2_spmd.clone.sunk | while | flops 278136320 | bytes 12588737 | solution.py:72
  22.6 2.0 gather_fusion
  24.6 2.7 %fusion.70 = bf16[32,128,256]{2,1,0:T(8,128)(2,1)S(1)} fusion(bf16[32,128,256]{2,1,0:T(8,128)(2,1)} %gather_fusion, pred[32]{0:T(512)(128)(4,1)S(1)} %get-tuple-element.273, bf16[2,32,128,128]{3,2,1,0:T(8,128)(2,1)} %get-tuple-element.310, s32[]{:T(128)S(6)} %select_n.142), kind=kOutput, calls=%fused_computation.6.clone.1 | convolution fusion | flops 269484032 | bytes 5242916 | tf_op jit(solution)/shard_map/while/body/eval_jaxpr/sij,sjf->sif/dot_general | solution.py:55
  32.6 2.0 gather_fusion
  34.6 2.7 %fusion.70 = bf16[32,128,256]{2,1,0:T(8,128)(2,1)S(1)} fusion(bf16[32,128,256]{2,1,0:T(8,128)(2,1)} %gather_fusion, pred[32]{0:T(512)(128)(4,1)S(1)} %get-tuple-element.273, bf16[2,32,128,128]{3,2,1,0:T(8,128)(2,1)} %get-tuple-element.310, s32[]{:T(128)S(6)} %select_n.142), kind=kOutput, calls=%fused_computation.6.clone.1 | convolution fusion | flops 269484032 | bytes 5242916 | tf_op jit(solution)/shard_map/while/body/eval_jaxpr/sij,sjf->sif/dot_general | solution.py:55
  41.1 23.0 %reduce-scatter.3.cloned.1.call-done = f32[128,256]{1,0:T(8,128)} async-done(((f32[512,256]{1,0:T(8,128)}), f32[128,256]{1,0:T(8,128)}) %reduce-scatter.3.cloned.1.call-update) | async-done | bytes 131088 | tf_op jit(solution)/shard_map/reduce_scatter | solution.py:78
  66.3 1.8 collective-permute-done.2
  68.3 1.5 collective-permute-start.3
  70.1 2.6 %collective-permute-done.3 = bf16[128,256]{1,0:T(8,128)(2,1)S(1)} collective-permute-done((bf16[128,256]{1,0:T(8,128)(2,1)S(1)}, bf16[128,256]{1,0:T(8,128)(2,1)S(1)}, u32[]{:S(2)}, u32[]{:S(2)}) %collective-permute-start.3) | collective-permute-done | bytes 65568 | tf_op jit(solution)/shard_map/ppermute | solution.py:12
  72.7 1.5 collective-permute-start.4
  75.1 2.6 %collective-permute-done.4 = bf16[256,256]{1,0:T(8,128)(2,1)S(1)} collective-permute-done((bf16[256,256]{1,0:T(8,128)(2,1)S(1)}, bf16[256,256]{1,0:T(8,128)(2,1)S(1)}, u32[]{:S(2)}, u32[]{:S(2)}) %collective-permute-start.4) | collective-permute-done | bytes 131104 | tf_op jit(solution)/shard_map/ppermute | solution.py:12
  77.8 20.1 %while.23 = (s32[]{:T(128)}, f32[4,128,256]{2,0,1:T(4,128)S(1)}, s32[2]{0:T(128)S(1)}, s32[2,32,2]{1,2,0:T(2,128)S(1)}, s32[]{:T(128)}, /*index=5*/bf16[2,32,128...) while((s32[]{:T(128)}, f32[4,128,256]{2,0,1:T(4,128)S(1)}, ...), condition=%wide.region_5.7_spmd.clone, body=%wide.region_4.6_spmd.clone.sunk | while | flops 278136320 | bytes 12588737 | solution.py:72
  80.4 2.0 gather_fusion.1
  82.4 2.7 %fusion.76 = bf16[32,128,256]{2,1,0:T(8,128)(2,1)S(1)} fusion(bf16[32,128,256]{2,1,0:T(8,128)(2,1)} %gather_fusion.1, pred[32]{0:T(512)(128)(4,1)S(1)} %get-tuple-element.282, bf16[2,32,128,128]{3,2,1,0:T(8,128)(2,1)} %get-tuple-element.343, s32[]{:T(128)S(6)} %select_n.144), kind=kOutput, calls=%fused_computation.28.clone.1 | convolution fusion | flops 269484032 | bytes 5242916 | tf_op jit(solution)/shard_map/while/body/eval_jaxpr/sij,sjf->sif/dot_general | solution.py:55
  90.5 2.0 gather_fusion.1
  92.5 2.7 %fusion.76 = bf16[32,128,256]{2,1,0:T(8,128)(2,1)S(1)} fusion(bf16[32,128,256]{2,1,0:T(8,128)(2,1)} %gather_fusion.1, pred[32]{0:T(512)(128)(4,1)S(1)} %get-tuple-element.282, bf16[2,32,128,128]{3,2,1,0:T(8,128)(2,1)} %get-tuple-element.343, s32[]{:T(128)S(6)} %select_n.144), kind=kOutput, calls=%fused_computation.28.clone.1 | convolution fusion | flops 269484032 | bytes 5242916 | tf_op jit(solution)/shard_map/while/body/eval_jaxpr/sij,sjf->sif/dot_general | solution.py:55
  96.5 1.4 fusion.77
  98.9 80.6 %all-reduce.2.cloned.1.call-done = f32[256,256]{0,1:T(8,128)} async-done(((f32[256,256]{0,1:T(8,128)}), f32[256,256]{0,1:T(8,128)}) %all-reduce.2.cloned.1.call-update) | async-done | bytes 262160 | tf_op jit(solution)/shard_map/psum | solution.py:103
  181.3 21.3 %reduce-scatter.5.cloned.1.call-done = f32[128,256]{1,0:T(8,128)} async-done(((f32[512,256]{1,0:T(8,128)}), f32[128,256]{1,0:T(8,128)}) %reduce-scatter.5.cloned.1.call-update) | async-done | bytes 131088 | tf_op jit(solution)/shard_map/reduce_scatter | solution.py:78
  202.5 1.5 select_bitcast_fusion
  (62 shorter events, 18.9 us)
Async XLA Ops:
  7.2 1.0 copy-start
  7.2 56.9 %reduce-scatter.3.cloned.1.call-start = ((), (), s32[]{:S(2)}) async-start(), calls=%async_computation.2 | async-start | bytes 655360 | tf_op jit(solution)/shard_map/reduce_scatter | solution.py:78
  8.3 5.9 %collective-permute-start = (bf16[128,256]{1,0:T(8,128)(2,1)S(1)}, bf16[128,256]{1,0:T(8,128)(2,1)S(1)}, u32[]{:S(2)}, u32[]{:S(2)}) collective-permute-start(bf16[128,256]{1,0:T(8,128)(2,1)S(1)} %convolution_convert_fusion.1), channel_id=1, source_target_pairs={{0,4},{4,0},{8,12},{12,8},{1,5},{5,1},{9,13},{13,9},{2,6},{6,2},{1... | collective-permute-start | bytes 196616 | tf_op jit(solution)/shard_map/ppermute | solution.py:12
  14.3 5.6 %collective-permute-start.1 = (bf16[256,256]{1,0:T(8,128)(2,1)S(1)}, bf16[256,256]{1,0:T(8,128)(2,1)S(1)}, u32[]{:S(2)}, u32[]{:S(2)}) collective-permute-start(bf16[256,256]{1,0:T(8,128)(2,1)S(1)} %maximum_select_fusion.2), channel_id=1, source_target_pairs={{0,8},{4,12},{8,0},{12,4},{1,9},{5,13},{9,1},{13,5},{2,10},{6,14},... | collective-permute-start | bytes 393224 | tf_op jit(solution)/shard_map/ppermute | solution.py:12
  40.1 29.8 %copy-start.2 = (bf16[1,128,256]{2,1,0:T(8,128)(2,1)S(1)}, bf16[1,128,256]{2,1,0:T(8,128)(2,1)}, u32[]{:S(2)}) copy-start(bf16[1,128,256]{2,1,0:T(8,128)(2,1)} %param.15) | copy-start | bytes 196612
  40.1 29.7 %copy-start.3 = (bf16[128,256]{1,0:T(8,128)(2,1)S(1)}, bf16[128,256]{1,0:T(8,128)(2,1)}, u32[]{:S(2)}) copy-start(bf16[128,256]{1,0:T(8,128)(2,1)} %param.13) | copy-start | bytes 196612
  41.0 138.4 %all-reduce.2.cloned.1.call-start = ((), (), s32[]{:S(2)}) async-start(), calls=%async_computation.3 | async-start | bytes 524288 | tf_op jit(solution)/shard_map/psum | solution.py:103
  65.0 3.1 %collective-permute-start.2 = (bf16[128,256]{1,0:T(8,128)(2,1)S(1)}, bf16[128,256]{1,0:T(8,128)(2,1)S(1)}, u32[]{:S(2)}, u32[]{:S(2)}) collective-permute-start(bf16[128,256]{1,0:T(8,128)(2,1)S(1)} %convert_element_type.15), channel_id=1, source_target_pairs={{16,0},{17,1},{18,2},{19,3},{20,4},{21,5},{22,6},{23,7},{24,8},{25... | collective-permute-start | bytes 196616 | tf_op jit(solution)/shard_map/ppermute | solution.py:23
  68.3 4.3 %collective-permute-start.3 = (bf16[128,256]{1,0:T(8,128)(2,1)S(1)}, bf16[128,256]{1,0:T(8,128)(2,1)S(1)}, u32[]{:S(2)}, u32[]{:S(2)}) collective-permute-start(bf16[128,256]{1,0:T(8,128)(2,1)S(1)} %convolution_convert_fusion), channel_id=1, source_target_pairs={{0,4},{4,0},{8,12},{12,8},{1,5},{5,1},{9,13},{13,9},{2,6},{6,2},{1... | collective-permute-start | bytes 196616 | tf_op jit(solution)/shard_map/ppermute | solution.py:12
  72.7 5.0 %collective-permute-start.4 = (bf16[256,256]{1,0:T(8,128)(2,1)S(1)}, bf16[256,256]{1,0:T(8,128)(2,1)S(1)}, u32[]{:S(2)}, u32[]{:S(2)}) collective-permute-start(bf16[256,256]{1,0:T(8,128)(2,1)S(1)} %maximum_select_fusion.3), channel_id=1, source_target_pairs={{0,8},{4,12},{8,0},{12,4},{1,9},{5,13},{9,1},{13,5},{2,10},{6,14},... | collective-permute-start | bytes 393224 | tf_op jit(solution)/shard_map/ppermute | solution.py:12
  75.1 127.4 %reduce-scatter.5.cloned.1.call-start = ((), (), s32[]{:S(2)}) async-start(), calls=%async_computation.4 | async-start | bytes 655360 | tf_op jit(solution)/shard_map/reduce_scatter | solution.py:78
  98.0 104.6 %copy-start.1 = (f32[128,256]{1,0:T(8,128)S(1)}, f32[128,256]{1,0:T(8,128)}, u32[]{:S(2)}) copy-start(f32[128,256]{1,0:T(8,128)} %reduce-scatter.3.cloned.1.call-done) | copy-start | bytes 393220
Sparse Core Ops, SparseCore 0:
  41.2 22.8 reduce-scatter.2
  75.2 104.2 all-reduce.1
  181.8 20.6 reduce-scatter.4
